TPU v7x, 32 devices: a whole 2x2x4 slice. The times are simulated.
32 devices in a mesh: groups: 2 (over y), seq: 4 (over z), fsdp: 4 (over x, core).
Axes of the slice: x: 2, y: 2, z: 4, core: 2. Of those that a mesh axis runs over, the one named last changes fastest.
Arguments:
- tokens: bfloat16 [1024, 1024], P(('groups', 'seq')), parts along dimension 0, may hold values from -16 to 16
- qkv_weight: bfloat16 [1024, 1536], P('seq', 'fsdp'), may hold values from -0.125 to 0.125
- covisible: int32 [8, 4], P('groups'), parts along dimension 0, may hold values 0 or 1
- block_drive: int32 [8], P('groups'), parts along dimension 0, may hold values from 0 to 2
- grad_out: bfloat16 [1024, 512], P(('groups', 'seq'), 'fsdp'), parts along dimension 0, may hold values from -6 to 6
Outputs:
- attention: bfloat16 [1024, 512], P(('groups', 'seq'), 'fsdp'), parts along dimension 0
- grad_input: bfloat16 [1024, 1024], P(('groups', 'seq'), 'fsdp'), parts along dimension 0
- grad_weight: float32 [2048, 1536], P(('groups', 'seq'), 'fsdp'), parts along dimension 0
There are 2 independent parts, one for each index of `groups`. A program takes and returns all parts, laid end to end along the dimension named above; an argument that names none is the same for every part. Nothing has to cross between parts.
All inputs are finite; a program needn't handle non-finite values.
Results may differ from a plain program's by a relative error of at most 0.018.
The roundings to bfloat16 on the way count: a program that leaves them out, or rounds other values in their place, can miss the bound.
Values may be sent and summed in bfloat16 or wider, within the bound.
No kernel may reach another device: no remote copies, remote signals or barrier semaphores. Data moves between devices by JAX's collectives and lax.ppermute only.
A program may use at most 64 MiB of HBM per device.

v0:
```python
import jax
import jax.numpy as jnp
from jax import lax
from jax.sharding import PartitionSpec as P

HD = 64
BLOCK = 128
MASKED_SCORE = -1e30


def query_visible(covisible, block_drive, first_block, block_count):
    own_rows = lax.dynamic_slice_in_dim(covisible, first_block, block_count, 0)
    own_drive = lax.dynamic_slice_in_dim(block_drive, first_block, block_count, 0)
    joined = jnp.logical_or(own_rows == 1, own_drive[:, None] == block_drive[None, :])
    return joined.astype(jnp.float32)


def key_visible(covisible, block_drive, first_block, block_count):
    own_columns = lax.dynamic_slice_in_dim(covisible, first_block, block_count, 1)
    own_drive = lax.dynamic_slice_in_dim(block_drive, first_block, block_count, 0)
    joined = jnp.logical_or(own_columns == 1, block_drive[:, None] == own_drive[None, :])
    return joined.astype(jnp.float32)


def block_onehot(length, block_total):
    member = lax.iota(jnp.int32, length) // BLOCK
    return (member[:, None] == lax.iota(jnp.int32, block_total)[None, :]).astype(jnp.float32)


def per_device(tokens, qkv_weight, covisible, block_drive, grad_out):
    local_rows = tokens.shape[0]
    seq_count = lax.axis_size("seq")
    seq_index = lax.axis_index("seq")
    out_width = qkv_weight.shape[1]
    local_heads = out_width // (3 * HD)
    block_count = local_rows // BLOCK
    block_total = covisible.shape[0]
    first_block = seq_index * block_count
    scaling = HD ** (-0.5)
    rows_visible = query_visible(covisible, block_drive, first_block, block_count)
    columns_visible = key_visible(covisible, block_drive, first_block, block_count)
    inputs = tokens
    projected = jnp.dot(
        inputs,
        lax.all_gather(qkv_weight, "seq", axis=0, tiled=True),
        preferred_element_type=jnp.float32,
    )
    projected = projected.astype(jnp.bfloat16).reshape(local_rows, local_heads, 3, HD)
    queries = projected[:, :, 0, :]
    local_keys = projected[:, :, 1, :]
    local_values = projected[:, :, 2, :]
    key_value = projected[:, :, 1:, :].reshape(local_rows, local_heads * 2 * HD)

    def local_visible(length):
        onehot = block_onehot(length, block_total)
        return (jnp.repeat(jnp.dot(rows_visible, onehot.T), BLOCK, axis=0) > 0.5)[None]

    panel = lax.all_gather(key_value, "seq", axis=0, tiled=True)
    running_max = jnp.full((local_heads, local_rows), MASKED_SCORE, jnp.float32)
    length = panel.shape[0]
    visible = local_visible(length)
    split_panel = panel.reshape(length, local_heads, 2, HD)
    scores = (
        jnp.einsum(
            "qhd,khd->hqk", queries, split_panel[:, :, 0, :], preferred_element_type=jnp.float32
        )
        * scaling
    )
    new_max = jnp.maximum(running_max, jnp.where(visible, scores, MASKED_SCORE).max(axis=2))
    shifted = jnp.exp(jnp.where(visible, scores - new_max[:, :, None], MASKED_SCORE))
    running_sum = shifted.sum(axis=2)
    wide_values = split_panel[:, :, 1, :].astype(jnp.float32)
    weighted = jnp.einsum(
        "hqk,khd->hqd",
        shifted,
        wide_values,
        precision=lax.Precision.HIGHEST,
        preferred_element_type=jnp.float32,
    )
    running_max, running_sum, weighted = (new_max, running_sum, weighted)
    attention_heads = (weighted / running_sum[:, :, None]).astype(jnp.bfloat16)
    attention = jnp.transpose(attention_heads, (1, 0, 2)).reshape(local_rows, local_heads * HD)
    log_total = running_max + jnp.log(running_sum)
    grad_heads = grad_out.reshape(local_rows, local_heads, HD)
    grad_dot_rows = jnp.sum(
        grad_heads.astype(jnp.float32)
        * attention.reshape(local_rows, local_heads, HD).astype(jnp.float32),
        axis=2,
    )
    grad_dot = jnp.transpose(grad_dot_rows)
    log_total_rows = jnp.transpose(log_total)
    all_log_total, all_grad_dot = (
        lax.all_gather(log_total_rows, "seq", axis=0, tiled=True),
        lax.all_gather(grad_dot_rows, "seq", axis=0, tiled=True),
    )
    query_rows = queries.reshape(local_rows, local_heads * HD)
    far_queries = lax.all_gather(query_rows, "seq", axis=0, tiled=True)
    far_grads = lax.all_gather(grad_out, "seq", axis=0, tiled=True)
    length = far_queries.shape[0]
    onehot = block_onehot(length, block_total)
    visible = (jnp.repeat(jnp.dot(onehot, columns_visible), BLOCK, axis=1) > 0.5)[None]
    far_heads = far_queries.reshape(length, local_heads, HD)
    far_grad_heads = far_grads.reshape(length, local_heads, HD)
    far_log_total = jnp.transpose(all_log_total)
    far_grad_dot = jnp.transpose(all_grad_dot)
    scores = (
        jnp.einsum("qhd,khd->hqk", far_heads, local_keys, preferred_element_type=jnp.float32)
        * scaling
    )
    probabilities = jnp.exp(jnp.where(visible, scores - far_log_total[:, :, None], MASKED_SCORE))
    grad_prob = jnp.einsum(
        "qhd,khd->hqk", far_grad_heads, local_values, preferred_element_type=jnp.float32
    )
    grad_score = (probabilities * (grad_prob - far_grad_dot[:, :, None]) * scaling).astype(
        jnp.bfloat16
    )
    grad_keys = jnp.einsum(
        "hqk,qhd->khd", grad_score, far_heads, preferred_element_type=jnp.float32
    )
    grad_values = jnp.einsum(
        "hqk,qhd->khd",
        probabilities.astype(jnp.bfloat16),
        far_grad_heads,
        preferred_element_type=jnp.float32,
    )
    grad_keys, grad_values = (grad_keys, grad_values)
    panel = lax.all_gather(key_value, "seq", axis=0, tiled=True)
    length = panel.shape[0]
    visible = local_visible(length)
    split_panel = panel.reshape(length, local_heads, 2, HD)
    panel_keys = split_panel[:, :, 0, :]
    scores = (
        jnp.einsum("qhd,khd->hqk", queries, panel_keys, preferred_element_type=jnp.float32)
        * scaling
    )
    probabilities = jnp.exp(jnp.where(visible, scores - log_total[:, :, None], MASKED_SCORE))
    grad_prob = jnp.einsum(
        "qhd,khd->hqk", grad_heads, split_panel[:, :, 1, :], preferred_element_type=jnp.float32
    )
    grad_score = (probabilities * (grad_prob - grad_dot[:, :, None]) * scaling).astype(jnp.bfloat16)
    grad_queries = jnp.einsum(
        "hqk,khd->qhd", grad_score, panel_keys, preferred_element_type=jnp.float32
    )
    grad_qkv = (
        jnp.stack([grad_queries, grad_keys, grad_values], axis=2)
        .astype(jnp.bfloat16)
        .reshape(local_rows, out_width)
    )
    partial_input = lax.dot_general(
        grad_qkv,
        lax.all_gather(qkv_weight, "seq", axis=0, tiled=True),
        (((1,), (1,)), ((), ())),
        preferred_element_type=jnp.float32,
    )
    grad_input = lax.psum_scatter(partial_input, "fsdp", scatter_dimension=1, tiled=True).astype(
        jnp.bfloat16
    )
    token_scale = (local_rows * seq_count) ** (-0.5)
    column_tokens = lax.all_to_all(tokens, "seq", split_axis=1, concat_axis=0, tiled=True)
    inputs = column_tokens
    summed_rows = lax.dot_general(
        inputs,
        lax.all_gather(grad_qkv, "seq", axis=0, tiled=True),
        (((0,), (0,)), ((), ())),
        preferred_element_type=jnp.float32,
    )
    grad_weight = summed_rows * token_scale
    return (attention, grad_input, grad_weight)


def solution(mesh):
    in_specs = (
        P(("groups", "seq"), None),
        P("seq", "fsdp"),
        P("groups", None),
        P("groups"),
        P(("groups", "seq"), "fsdp"),
    )
    out_specs = (
        P(("groups", "seq"), "fsdp"),
        P(("groups", "seq"), "fsdp"),
        P(("groups", "seq"), "fsdp"),
    )
    return jax.shard_map(
        per_device, mesh=mesh, in_specs=in_specs, out_specs=out_specs, check_vma=False
    )
```

profile of v0, /device:TPU:0, one launch (start us, length us, event | category | flops | bytes accessed | tf_op | source)
XLA Modules:
  0.0 121.6 jit_solution(15169649852441177908)
XLA Ops:
  7.2 0.0 reduce-scatter.2.cloned.1.call-start
  7.2 0.0 copy-start.3
  7.2 0.6 copy-done.3
  7.9 0.0 copy-start.2
  7.9 0.6 dynamic_slice.11
  8.5 0.1 copy-done.2
  8.6 0.9 fusion.35
  9.5 0.0 copy-start
  9.5 21.6 %all_gather.23 = bf16[1024,384]{1,0:T(8,128)(2,1)S(1)} all-gather(bf16[256,384]{1,0:T(8,128)(2,1)} %param.6), channel_id=1, replica_groups=mesh['groups'=2,'seq'=4,'fsdp'=4] {'seq'}, dimensions={0}, use_global_device_ids=true | all-gather | bytes 983040 | tf_op jit(solution)/shard_map/all_gather | solution.py:45
  31.1 0.0 copy-done
  31.1 0.3 convolution_convert_fusion
  31.4 0.1 copy.26
  31.6 12.8 %all_gather.24 = bf16[512,256]{0,1:T(8,128)(2,1)S(1)} all-gather(bf16[128,256]{0,1:T(8,128)(2,1)S(1)} %bitcast.145), channel_id=1, replica_groups=mesh['groups'=2,'seq'=4,'fsdp'=4] {'seq'}, dimensions={0}, use_global_device_ids=true | all-gather | bytes 327680 | tf_op jit(solution)/shard_map/all_gather | solution.py:58
  44.4 0.3 select_reduce_fusion
  44.7 0.2 fusion.24
  45.0 0.1 constant_dynamic-slice_fusion
  45.1 0.0 copy-start.1
  45.1 0.8 copy-done.1
  45.8 0.1 copy.30
  45.9 13.3 %all_gather.27 = bf16[512,128]{1,0:T(8,128)(2,1)S(1)} all-gather(bf16[128,128]{1,0:T(8,128)(2,1)S(1)} %copy-done.1), channel_id=1, replica_groups=mesh['groups'=2,'seq'=4,'fsdp'=4] {'seq'}, dimensions={0}, use_global_device_ids=true | all-gather | bytes 163840 | tf_op jit(solution)/shard_map/all_gather | solution.py:98
  59.3 8.2 %all_gather.26 = f32[512,2]{0,1:T(2,128)S(1)} all-gather(f32[128,2]{0,1:T(2,128)S(1)} %bitcast_add_fusion), channel_id=1, replica_groups=mesh['groups'=2,'seq'=4,'fsdp'=4] {'seq'}, dimensions={0}, use_global_device_ids=true | all-gather | bytes 5120 | tf_op jit(solution)/shard_map/all_gather | solution.py:93
  67.5 0.1 copy.46
  67.6 0.9 fusion.34
  68.5 12.3 %all_gather.25 = bf16[512,128]{0,1:T(8,128)(2,1)S(1)} all-gather(bf16[128,128]{0,1:T(8,128)(2,1)S(1)} %bitcast.146), channel_id=1, replica_groups=mesh['groups'=2,'seq'=4,'fsdp'=4] {'seq'}, dimensions={0}, use_global_device_ids=true | all-gather | bytes 163840 | tf_op jit(solution)/shard_map/all_gather | solution.py:97
  80.8 0.6 multiply_reduce_fusion
  81.3 8.0 %all_gather.28 = f32[512,2]{0,1:T(2,128)S(1)} all-gather(f32[128,2]{0,1:T(2,128)S(1)} %get-tuple-element.14), channel_id=1, replica_groups=mesh['groups'=2,'seq'=4,'fsdp'=4] {'seq'}, dimensions={0}, use_global_device_ids=true | all-gather | bytes 5120 | tf_op jit(solution)/shard_map/all_gather | solution.py:94
  89.4 0.1 copy.34
  89.5 0.4 fusion.6
  89.9 0.2 fusion.20
  90.1 0.4 fusion.19
  90.5 0.5 fusion.18
  91.0 1.2 fusion.62
  92.2 0.0 reduce-scatter.2.cloned.1.call-update
  92.2 0.8 copy.37
  93.0 3.4 %all-to-all-start = ((bf16[128,4,256]{0,2,1:T(8,128)(2,1)}), bf16[128,4,256]{0,2,1:T(8,128)(2,1)S(1)}, u32[]{:S(2)}, u32[]{:S(2)}) async-start(bf16[128,4,256]{0,2,1:T(8,128)(2,1)} %bitcast.36), calls=%async_computation.1 | async-start | bytes 524288 | tf_op jit(solution)/shard_map/all_to_all | solution.py:159
  96.5 0.7 copy.39
  97.2 14.2 %all_gather.29 = bf16[512,384]{0,1:T(8,128)(2,1)S(1)} all-gather(bf16[128,384]{0,1:T(8,128)(2,1)S(1)} %bitcast.134), channel_id=1, replica_groups=mesh['groups'=2,'seq'=4,'fsdp'=4] {'seq'}, dimensions={0}, use_global_device_ids=true | all-gather | bytes 491520 | tf_op jit(solution)/shard_map/all_gather | solution.py:163
  111.4 0.0 all-to-all-done
  111.4 0.1 copy.38
  111.6 0.3 fusion.11
  111.8 0.9 copy.40
  112.7 0.5 reduce-scatter.2.cloned.1.call-done
  113.2 1.5 %convert_element_type.44 = bf16[128,256]{1,0:T(8,128)(2,1)} convert(f32[128,256]{1,0:T(8,128)} %reduce-scatter.2.cloned.1.call-done) | non-fusion elementwise | flops 32768 | bytes 196608 | tf_op jit(solution)/shard_map/convert_element_type | solution.py:155
  (10 shorter events, 0.1 us)
Async XLA Ops:
  7.2 106.1 %reduce-scatter.2.cloned.1.call-start = ((), (), s32[]{:S(2)}) async-start(), calls=%async_computation.2 | async-start | bytes 655360 | tf_op jit(solution)/shard_map/reduce_scatter | solution.py:155
  7.2 0.7 copy-start.3
  7.9 0.7 copy-start.2
  9.5 21.6 %copy-start = (bf16[128,1024]{1,0:T(8,128)(2,1)S(1)}, bf16[128,1024]{1,0:T(8,128)(2,1)}, u32[]{:S(2)}) copy-start(bf16[128,1024]{1,0:T(8,128)(2,1)} %param.5) | copy-start | bytes 786436
  45.1 0.8 copy-start.1
  93.0 18.4 %all-to-all-start = ((bf16[128,4,256]{0,2,1:T(8,128)(2,1)}), bf16[128,4,256]{0,2,1:T(8,128)(2,1)S(1)}, u32[]{:S(2)}, u32[]{:S(2)}) async-start(bf16[128,4,256]{0,2,1:T(8,128)(2,1)} %bitcast.36), calls=%async_computation.1 | async-start | bytes 524288 | tf_op jit(solution)/shard_map/all_to_all | solution.py:159
Sparse Core Ops, SparseCore 0:
  92.3 20.8 reduce-scatter.1
where the time goes:
time: 122 us
  blocking collectives  90.5 us (74%)
  between operations  14.2 us (12%)
  matrix products  5.87 us (5%)
  local copies, waits for them, and re-layouts  5.24 us (4%)
  starting transfers between devices  3.44 us (3%)
  other arithmetic  1.84 us (2%)
    all_gather x1, blocking collectives, per_device(): lax.all_gather(qkv_weight, 'seq', axis=0, tiled=True)  21.6 us
    all_gather x1, blocking collectives, per_device(): lax.all_gather(grad_qkv, 'seq', axis=0, tiled=True)  14.2 us
    all_gather x1, blocking collectives, per_device(): far_grads = lax.all_gather(grad_out, 'seq', axis=0, tiled=True)  13.3 us
    all_gather x1, blocking collectives, per_device(): panel = lax.all_gather(key_value, 'seq', axis=0, tiled=True)  12.8 us
    all_gather x1, blocking collectives, per_device(): far_queries = lax.all_gather(query_rows, 'seq', axis=0, tiled=True)  12.3 us
    all_gather x1, blocking collectives, per_device(): lax.all_gather(log_total_rows, 'seq', axis=0, tiled=True)  8.22 us
    all_gather x1, blocking collectives, per_device(): lax.all_gather(grad_dot_rows, 'seq', axis=0, tiled=True)  8.03 us
    unnamed x13, local copies, waits for them, and re-layouts  4.19 us
  transfers between devices with their start and end apart: 2, of which 1 were waited for; matrix products, arithmetic and copies ran while one was open for 2% of the time, Pallas kernels for 0%

commit v1 on v0

--- a/solution.py
+++ b/solution.py
@@ -94,8 +94,14 @@
         lax.all_gather(grad_dot_rows, "seq", axis=0, tiled=True),
     )
     query_rows = queries.reshape(local_rows, local_heads * HD)
-    far_queries = lax.all_gather(query_rows, "seq", axis=0, tiled=True)
-    far_grads = lax.all_gather(grad_out, "seq", axis=0, tiled=True)
+
+    def _run_circles(field, tile_in, link_axis):
+        right_arr = jnp.concatenate([field, tile_in], axis=1)
+        far_arr = lax.all_gather(right_arr, axis_name=link_axis, axis=0, tiled=True)
+        q_next = jnp.split(far_arr, [field.shape[1]], axis=1)
+        return q_next
+
+    far_queries, far_grads = _run_circles(query_rows, grad_out, "seq")
     length = far_queries.shape[0]
     onehot = block_onehot(length, block_total)
     visible = (jnp.repeat(jnp.dot(onehot, columns_visible), BLOCK, axis=1) > 0.5)[None]

time: 122 us -> 111 us (0.910)
  blocking collectives: 90.5 us -> 79.7 us
    all_gather x2 -> x1, blocking collectives: 25.6 us -> 13.8 us  [_run_circles(): far_arr = lax.all_gather(right_arr, axis_name=link_axis, axis=0, tiled=True)]
  transfers between devices with their start and end apart: 2 -> 2, of which waited for: 1 -> 0; matrix products, arithmetic and copies ran while one was open for 2% -> 3% of each run, Pallas kernels for 0% -> 0%
where the time goes in v1:
time: 111 us
  blocking collectives  79.7 us (72%)
  between operations  14.2 us (13%)
  matrix products  5.87 us (5%)
  local copies, waits for them, and re-layouts  5.49 us (5%)
  starting transfers between devices  3.45 us (3%)
  other arithmetic  1.85 us (2%)
    all_gather x1, blocking collectives, per_device(): lax.all_gather(qkv_weight, 'seq', axis=0, tiled=True)  21.6 us
    all_gather x1, blocking collectives, per_device(): lax.all_gather(grad_qkv, 'seq', axis=0, tiled=True)  14.2 us
    all_gather x1, blocking collectives, _run_circles(): far_arr = lax.all_gather(right_arr, axis_name=link_axis, axis=0, tiled=True)  13.8 us
    all_gather x1, blocking collectives, per_device(): panel = lax.all_gather(key_value, 'seq', axis=0, tiled=True)  12.8 us
    all_gather x1, blocking collectives, per_device(): lax.all_gather(grad_dot_rows, 'seq', axis=0, tiled=True)  9.21 us
    all_gather x1, blocking collectives, per_device(): lax.all_gather(log_total_rows, 'seq', axis=0, tiled=True)  8.07 us
    unnamed x13, local copies, waits for them, and re-layouts  4.19 us
    all_to_all x1, starting transfers between devices, per_device(): lax.all_to_all(tokens, 'seq', split_axis=1, concat_axis=0, tiled=True)  3.41 us
  transfers between devices with their start and end apart: 2, of which 0 were waited for; matrix products, arithmetic and copies ran while one was open for 3% of the time, Pallas kernels for 0%

profile of v1, /device:TPU:0, one launch (start us, length us, event | category | flops | bytes accessed | tf_op | source)
XLA Modules:
  0.0 110.6 jit_solution(4485363590695219461)
XLA Ops:
  7.2 0.0 reduce-scatter.2.cloned.1.call-start
  7.2 0.0 copy-start.3
  7.2 0.6 copy-done.3
  7.9 0.0 copy-start.2
  7.9 0.6 dynamic_slice.11
  8.5 0.1 copy-done.2
  8.6 0.9 fusion.34
  9.5 0.0 copy-start
  9.5 21.6 %all_gather.20 = bf16[1024,384]{1,0:T(8,128)(2,1)S(1)} all-gather(bf16[256,384]{1,0:T(8,128)(2,1)} %param.6), channel_id=1, replica_groups=mesh['groups'=2,'seq'=4,'fsdp'=4] {'seq'}, dimensions={0}, use_global_device_ids=true | all-gather | bytes 983040 | tf_op jit(solution)/shard_map/all_gather | solution.py:45
  31.1 0.0 copy-done
  31.1 0.3 convolution_convert_fusion
  31.4 0.1 copy.30
  31.6 12.8 %all_gather.21 = bf16[512,256]{0,1:T(8,128)(2,1)S(1)} all-gather(bf16[128,256]{0,1:T(8,128)(2,1)S(1)} %bitcast.131), channel_id=1, replica_groups=mesh['groups'=2,'seq'=4,'fsdp'=4] {'seq'}, dimensions={0}, use_global_device_ids=true | all-gather | bytes 327680 | tf_op jit(solution)/shard_map/all_gather | solution.py:58
  44.3 0.3 select_reduce_fusion
  44.7 0.2 fusion.23
  45.0 0.1 constant_dynamic-slice_fusion
  45.1 0.0 copy-start.1
  45.1 0.8 copy-done.1
  45.8 0.1 copy.34
  45.9 8.1 %all_gather.23 = f32[512,2]{0,1:T(2,128)S(1)} all-gather(f32[128,2]{0,1:T(2,128)S(1)} %bitcast_add_fusion), channel_id=1, replica_groups=mesh['groups'=2,'seq'=4,'fsdp'=4] {'seq'}, dimensions={0}, use_global_device_ids=true | all-gather | bytes 5120 | tf_op jit(solution)/shard_map/all_gather | solution.py:93
  54.0 0.1 copy.50
  54.1 0.9 fusion.33
  55.0 0.1 copy.36
  55.1 13.8 %all_gather.22 = bf16[512,256]{1,0:T(8,128)(2,1)S(1)} all-gather(bf16[128,256]{1,0:T(8,128)(2,1)S(1)} %pad_maximum_fusion.1), channel_id=1, replica_groups=mesh['groups'=2,'seq'=4,'fsdp'=4] {'seq'}, dimensions={0}, use_global_device_ids=true | all-gather | bytes 327680 | tf_op jit(solution)/shard_map/all_gather | solution.py:100
  69.0 0.1 copy.37
  69.1 0.6 multiply_reduce_fusion
  69.7 9.2 %all_gather.24 = f32[512,2]{0,1:T(2,128)S(1)} all-gather(f32[128,2]{0,1:T(2,128)S(1)} %get-tuple-element.16), channel_id=1, replica_groups=mesh['groups'=2,'seq'=4,'fsdp'=4] {'seq'}, dimensions={0}, use_global_device_ids=true | all-gather | bytes 5120 | tf_op jit(solution)/shard_map/all_gather | solution.py:94
  78.9 0.1 copy.40
  79.0 0.4 fusion.5
  79.4 0.2 fusion.19
  79.5 0.4 fusion.18
  80.0 0.5 fusion.17
  80.5 1.2 %fusion.62 = f32[128,1024]{1,0:T(8,128)} fusion(bf16[128,384]{0,1:T(8,128)(2,1)S(1)} %bitcast.119, bf16[1024,384]{1,0:T(8,128)(2,1)S(1)} %all_gather.20), kind=kOutput, calls=%fused_computation.92 | convolution fusion | flops 100663296 | bytes 1409024 | tf_op jit(solution)/shard_map/dot_general | solution.py:155
  81.7 0.0 reduce-scatter.2.cloned.1.call-update
  81.7 0.8 copy.42
  82.5 3.4 %all-to-all-start = ((bf16[128,4,256]{0,2,1:T(8,128)(2,1)}), bf16[128,4,256]{0,2,1:T(8,128)(2,1)S(1)}, u32[]{:S(2)}, u32[]{:S(2)}) async-start(bf16[128,4,256]{0,2,1:T(8,128)(2,1)} %bitcast.35), calls=%async_computation.1 | async-start | bytes 524288 | tf_op jit(solution)/shard_map/all_to_all | solution.py:165
  85.9 0.7 copy.44
  86.7 14.2 %all_gather.25 = bf16[512,384]{0,1:T(8,128)(2,1)S(1)} all-gather(bf16[128,384]{0,1:T(8,128)(2,1)S(1)} %bitcast.120), channel_id=1, replica_groups=mesh['groups'=2,'seq'=4,'fsdp'=4] {'seq'}, dimensions={0}, use_global_device_ids=true | all-gather | bytes 491520 | tf_op jit(solution)/shard_map/all_gather | solution.py:169
  100.9 0.0 all-to-all-done
  100.9 0.1 copy.43
  101.0 0.3 fusion.10
  101.3 0.9 copy.45
  102.2 0.0 reduce-scatter.2.cloned.1.call-done
  102.2 1.5 %convert_element_type.44 = bf16[128,256]{1,0:T(8,128)(2,1)} convert(f32[128,256]{1,0:T(8,128)} %reduce-scatter.2.cloned.1.call-done) | non-fusion elementwise | flops 32768 | bytes 196608 | tf_op jit(solution)/shard_map/convert_element_type | solution.py:161
  (12 shorter events, 0.1 us)
Async XLA Ops:
  7.2 95.1 %reduce-scatter.2.cloned.1.call-start = ((), (), s32[]{:S(2)}) async-start(), calls=%async_computation.2 | async-start | bytes 655360 | tf_op jit(solution)/shard_map/reduce_scatter | solution.py:161
  7.2 0.7 copy-start.3
  7.9 0.7 copy-start.2
  9.5 21.6 %copy-start = (bf16[128,1024]{1,0:T(8,128)(2,1)S(1)}, bf16[128,1024]{1,0:T(8,128)(2,1)}, u32[]{:S(2)}) copy-start(bf16[128,1024]{1,0:T(8,128)(2,1)} %param.5) | copy-start | bytes 786436
  45.1 0.8 copy-start.1
  82.5 18.4 %all-to-all-start = ((bf16[128,4,256]{0,2,1:T(8,128)(2,1)}), bf16[128,4,256]{0,2,1:T(8,128)(2,1)S(1)}, u32[]{:S(2)}, u32[]{:S(2)}) async-start(bf16[128,4,256]{0,2,1:T(8,128)(2,1)} %bitcast.35), calls=%async_computation.1 | async-start | bytes 524288 | tf_op jit(solution)/shard_map/all_to_all | solution.py:165
Sparse Core Ops, SparseCore 0:
  81.8 19.8 reduce-scatter.1
